TPU v7x, 512 devices: a whole 4x4x16 slice. The times are simulated.
512 devices in a mesh: dom: 64 (over z_hi, x, y, core), lag: 8 (over z_lo).
Axes of the slice: x: 4, y: 4, z: 16 (z_hi: 2, z_lo: 8; z = z_hi * 8 + z_lo), core: 2. Of those that a mesh axis runs over, the one named last changes fastest.
Arguments:
- delayed_crowd_history: bfloat16 [8, 64, 2048, 128], P('lag', None, 'dom'), may hold values from -6 to 6
- predicted_crowd_array: bfloat16 [64, 2048, 128], P('lag', 'dom'), may hold values from -40 to 40
- probe_target_spot: int32 [1024, 256], P('dom'), may hold values from 0 to 255
- alive_probe_places: int32 [1024], P('dom'), may hold values from 64 to 256, as said below
- probed_heat_levels: float32 [1024, 256], P('dom'), may hold values from -6 to 6
- probe_reciprocal_spread: float32 [1024, 256], P('dom'), may hold values from 0.1 to 1.6
- decay_extent_squares: int32 [1024], P('dom'), may hold values from 16 to 32
Outputs:
- smoothed: bfloat16 [8, 64, 2048, 128], P('lag', None, 'dom')
Inputs may be any that keep to these rules, and one draw needn't show every extreme that they name: `alive_probe_places`: live observations of a patch occupy its first slots.
All inputs are finite; a program needn't handle non-finite values.
Results may differ from a plain program's by a relative error of at most 0.0062.
Values may be sent and summed in bfloat16 or wider, within the bound.
A program may use at most 64 MiB of HBM per device.

v0:
```python
import jax
import jax.numpy as jnp
from jax import lax
from jax.sharding import PartitionSpec as P

PATCH = 16
NS_STEPS = 4
REACH = 2


def padded_2(block, sides, width):
    for axis, dim in sides:
        count = lax.axis_size(axis)
        forward = [(i, i + 1) for i in range(count - 1)]
        backward = [(target, source) for source, target in forward]
        low = lax.ppermute(
            lax.slice_in_dim(block, block.shape[dim] - width, None, axis=dim), axis, forward
        )
        high = lax.ppermute(lax.slice_in_dim(block, 0, width, axis=dim), axis, backward)
        block = jnp.concatenate([low, block, high], axis=dim)
    return block


def inverse_root(gram_part, right_side):
    crowd_members_number = gram_part.shape[-1]
    identity = jnp.eye(crowd_members_number, dtype=jnp.float32)
    frobenius = jnp.sqrt(jnp.sum(gram_part * gram_part, axis=(1, 2)))
    bound_value = crowd_members_number - 1.0 + frobenius
    iterate = (gram_part + (crowd_members_number - 1.0) * identity) / bound_value[:, None, None]
    root_iter = jnp.broadcast_to(identity, gram_part.shape)
    for sweep_index in range(NS_STEPS):
        correction = 1.5 * identity - 0.5 * jnp.matmul(
            root_iter, iterate, precision=lax.Precision.HIGHEST
        )
        iterate = jnp.matmul(iterate, correction, precision=lax.Precision.HIGHEST)
        root_iter = jnp.matmul(correction, root_iter, precision=lax.Precision.HIGHEST)
    inner_prod = jnp.matmul(root_iter, right_side[:, :, None], precision=lax.Precision.HIGHEST)
    mean_weights = (
        jnp.matmul(root_iter, inner_prod, precision=lax.Precision.HIGHEST)[:, :, 0]
        / bound_value[:, None]
    )
    spread = jnp.sqrt(crowd_members_number - 1.0) / jnp.sqrt(bound_value)
    return (spread[:, None, None] * root_iter + mean_weights[:, :, None]).astype(jnp.bfloat16)


def local_gram(padded, radius, crowd_members_number, patch_rows, patch_cols):
    group_size = padded.shape[3]
    reach_width = 2 * REACH + 1
    col_base = jnp.repeat(
        (jnp.arange(reach_width, dtype=jnp.int32) - REACH) * PATCH, group_size
    ).astype(jnp.float32)
    gram_sum = jnp.zeros(
        (patch_rows, patch_cols, crowd_members_number, crowd_members_number), jnp.float32
    )
    right_side = jnp.zeros((patch_rows, patch_cols, crowd_members_number), jnp.float32)
    for shift_row in range(reach_width):
        pieces = [
            padded[:, shift_row : shift_row + patch_rows, shift_col : shift_col + patch_cols, :]
            for shift_col in range(reach_width)
        ]
        stacked = jnp.concatenate(pieces, axis=3)
        anomaly_near = stacked[:crowd_members_number]
        weight_near = stacked[crowd_members_number].astype(jnp.float32)
        innov_near = stacked[crowd_members_number + 1].astype(jnp.float32)
        row_offset = (
            (shift_row - REACH) * PATCH
            + stacked[crowd_members_number + 2].astype(jnp.float32)
            - 7.5
        )
        col_offset = col_base + stacked[crowd_members_number + 3].astype(jnp.float32) - 7.5
        taper_weight = jnp.square(
            jnp.maximum(
                0.0, 1.0 - (jnp.square(row_offset) + jnp.square(col_offset)) / jnp.square(radius)
            )
        )
        scaled = (taper_weight * weight_near * anomaly_near.astype(jnp.float32)).astype(
            jnp.bfloat16
        )
        weighted = (taper_weight * innov_near).astype(jnp.bfloat16)
        gram_sum = gram_sum + jnp.einsum(
            "mxyo,nxyo->xymn", scaled, anomaly_near, preferred_element_type=jnp.float32
        )
        right_side = right_side + jnp.einsum(
            "mxyo,xyo->xym", anomaly_near, weighted, preferred_element_type=jnp.float32
        )
    return (gram_sum, right_side)


def shards(
    delayed_crowd_history,
    predicted_crowd_array,
    probe_target_spot,
    alive_probe_places,
    probed_heat_levels,
    probe_reciprocal_spread,
    decay_extent_squares,
):
    lag_total = lax.axis_size("lag")
    lag_rank = lax.axis_index("lag")
    crowd_share_part, tile_vertical_extent, tile_lateral_extent = predicted_crowd_array.shape
    patch_rows = tile_vertical_extent // PATCH
    patch_cols = tile_lateral_extent // PATCH
    patch_total = patch_rows * patch_cols
    slot_count = probe_target_spot.shape[1]
    group_size = slot_count // lag_total
    index_patch = jnp.arange(patch_total, dtype=jnp.int32)
    lattice_node_place = (
        ((index_patch // patch_cols)[:, None] * PATCH + probe_target_spot // PATCH)
        * tile_lateral_extent
        + (index_patch % patch_cols)[:, None] * PATCH
        + probe_target_spot % PATCH
    )
    probed_markers = jnp.take(
        predicted_crowd_array.reshape(crowd_share_part, tile_vertical_extent * tile_lateral_extent),
        lattice_node_place.reshape(-1),
        axis=1,
    )
    probed_markers = probed_markers.reshape(crowd_share_part, patch_rows, patch_cols, slot_count)
    received = lax.all_to_all(probed_markers, "lag", split_axis=3, concat_axis=0, tiled=True)
    crowd_members_number = received.shape[0]
    average_reading = jnp.sum(received, axis=0, dtype=jnp.float32) / crowd_members_number
    obs_anomaly = (received.astype(jnp.float32) - average_reading).astype(jnp.bfloat16)
    slot_start = lag_rank * group_size

    def gather_fraction(table):
        piece = lax.dynamic_slice_in_dim(table, slot_start, group_size, 1)
        return piece.reshape(patch_rows, patch_cols, group_size)

    slot_index = slot_start + jnp.arange(group_size, dtype=jnp.int32)
    usable_entry = (slot_index[None, :] < alive_probe_places[:, None]).reshape(
        patch_rows, patch_cols, group_size
    )
    precision_share = gather_fraction(probe_reciprocal_spread)
    reading_fraction = gather_fraction(probed_heat_levels)
    cell_share = gather_fraction(probe_target_spot)
    obs_weight = jnp.where(usable_entry, precision_share, 0.0).astype(jnp.bfloat16)
    departure_vector = jnp.where(
        usable_entry, precision_share * (reading_fraction - average_reading), 0.0
    ).astype(jnp.bfloat16)
    placed = jnp.stack(
        [
            obs_weight,
            departure_vector,
            (cell_share // PATCH).astype(jnp.bfloat16),
            (cell_share % PATCH).astype(jnp.bfloat16),
        ],
        0,
    )
    combined = jnp.concatenate([obs_anomaly, placed], 0)
    extended = padded_2(combined, (("dom", 1),), REACH)
    padded = jnp.pad(extended, ((0, 0), (0, 0), (REACH, REACH), (0, 0)))
    radius = decay_extent_squares.reshape(patch_rows, patch_cols, 1).astype(jnp.float32)
    gram_sum, right_side = local_gram(padded, radius, crowd_members_number, patch_rows, patch_cols)
    gram_flat = gram_sum.reshape(patch_total, crowd_members_number, crowd_members_number)
    rhs_flat = right_side.reshape(patch_total, crowd_members_number)
    gram_all, rhs_all = lax.psum((gram_flat, rhs_flat), "lag")
    transform = inverse_root(gram_all, rhs_all)
    lag_state = delayed_crowd_history[0]
    lag_mean = jnp.sum(lag_state, axis=0, dtype=jnp.float32) / crowd_members_number
    lag_anomaly = (lag_state.astype(jnp.float32) - lag_mean).astype(jnp.bfloat16)
    patch_grid = lag_anomaly.reshape(crowd_members_number, patch_rows, PATCH, patch_cols, PATCH)
    mixing = transform.reshape(patch_rows, patch_cols, crowd_members_number, crowd_members_number)
    updated = jnp.einsum(
        "maibj,abmn->naibj", patch_grid, mixing, preferred_element_type=jnp.float32
    )
    result = (
        updated.reshape(crowd_members_number, tile_vertical_extent, tile_lateral_extent) + lag_mean
    )
    return result.astype(jnp.bfloat16)[None]


def solution(mesh):
    in_specs = (
        P("lag", None, "dom", None),
        P("lag", "dom", None),
        P("dom", None),
        P("dom"),
        P("dom", None),
        P("dom", None),
        P("dom"),
    )
    out_specs = P("lag", None, "dom", None)
    return jax.shard_map(shards, mesh=mesh, in_specs=in_specs, out_specs=out_specs, check_vma=False)
```

profile of v0, /device:TPU:2, one launch (start us, length us, event | category | flops | bytes accessed | tf_op | source)
XLA Modules:
  0.0 256.4 jit_solution(7928711825052308144)
XLA Ops:
  8.2 1.3 copy.242
  9.5 12.1 %gather_fusion = bf16[4096,8]{1,0:T(8,128)(2,1)S(1)} fusion(bf16[8,4096]{0,1:T(8,128)(2,1)S(1)} %bitcast.330, s32[4096]{0:T(1024)S(1)} %broadcast_clamp_fusion), kind=kCustom, calls=%fused_computation | custom fusion | bytes 147456 | tf_op jit(solution)/shard_map/jit(_take)/gather | solution.py:113
  21.6 1.5 copy.243
  24.7 1.7 reshape.455
  26.4 12.5 %all-to-all-start = ((bf16[8,2,2048]{2,1,0:T(2,128)(2,1)}), bf16[8,2,2048]{2,1,0:T(2,128)(2,1)S(1)}, u32[]{:S(2)}, u32[]{:S(2)}) async-start(bf16[8,2,2048]{2,1,0:T(2,128)(2,1)} %reshape.455), calls=%async_computation | async-start | bytes 131072 | tf_op jit(solution)/shard_map/all_to_all | solution.py:119
  42.3 7.5 %all-to-all-done = bf16[8,2,2048]{2,1,0:T(2,128)(2,1)S(1)} async-done(((bf16[8,2,2048]{2,1,0:T(2,128)(2,1)}), bf16[8,2,2048]{2,1,0:T(2,128)(2,1)S(1)}, u32[]{:S(2)}, u32[]{:S(2)}) %all-to-all-start) | async-done | bytes 65568 | tf_op jit(solution)/shard_map/all_to_all | solution.py:119
  51.0 2.0 convert_reduce_fusion
  54.7 1.9 collective-permute-start
  56.6 5.9 %collective-permute-start.1 = (bf16[68,2,8,32]{3,2,1,0:T(8,128)(2,1)S(1)}, bf16[68,2,8,32]{3,2,1,0:T(8,128)(2,1)S(1)}, u32[]{:S(2)}, u32[]{:S(2)}) collective-permute-start(bf16[68,2,8,32]{3,2,1,0:T(8,128)(2,1)S(1)} %constant_dynamic-update-slice_fusion), channel_id=1, source_target_pairs={{8,0},{16,8},{24,16},{32,24},{40,32},{48,40},{56,48},{64,56},{72,6... | collective-permute-start | bytes 208904 | tf_op jit(solution)/shard_map/ppermute | solution.py:19
  62.6 2.1 collective-permute-done
  64.7 1.8 collective-permute-done.1
  67.2 2.7 %fusion.164 = (bf16[68,2,8,32]{3,2,1,0:T(8,128)(2,1)}, bf16[68,2,8,32]{3,2,1,0:T(8,128)(2,1)}, bf16[68,2,8,32]{3,2,1,0:T(8,128)(2,1)}, bf16[68,2,8,32]{3,2,1,0:T...) fusion(bf16[68,6,12,32]{3,2,1,0:T(8,128)(2,1)S(1)} %fusion.5), kind=kLoop, calls=%fused_computation.253 | loop fusion | bytes 2646016 | tf_op jit(solution)/shard_map/slice | solution.py:58
  72.5 1.6 concatenate.29
  75.6 1.6 concatenate.31
  78.0 1.5 concatenate.32
  80.4 1.7 concatenate.34
  82.9 2.4 concatenate.35
  86.5 1.6 fusion.157
  94.2 1.3 fusion.23
  95.5 26.8 %psum.15 = f32[16,64]{1,0:T(8,128)S(1)} all-reduce(f32[16,64]{1,0:T(8,128)S(1)} %add_bitcast_fusion), channel_id=1, replica_groups=mesh['dom'=64,'lag'=8] {'lag'}, use_global_device_ids=true, to_apply=%region_4.5 | all-reduce | flops 1024 | bytes 8192 | tf_op jit(solution)/shard_map/psum | solution.py:156
  122.3 111.9 %all-reduce.3.cloned.1.call-done = f32[16,64,64]{2,1,0:T(8,128)} async-done(((f32[16,64,64]{2,1,0:T(8,128)}), f32[16,64,64]{2,1,0:T(8,128)}) %all-reduce.3.cloned.1.call-update) | async-done | bytes 262160 | tf_op jit(solution)/shard_map/psum | solution.py:156
  234.2 1.3 multiply_reduce_fusion
  235.5 1.7 fusion.9
  247.9 1.6 copy.266
  (114 shorter events, 34.2 us)
Async XLA Ops:
  23.1 15.8 %copy-start.15 = (s32[16]{0:T(128)S(1)}, s32[16]{0:T(128)}, u32[]{:S(2)}) copy-start(s32[16]{0:T(128)} %param.13) | copy-start | bytes 196
  23.1 15.8 %copy-start.7 = (bf16[1,64,32,128]{3,2,1,0:T(8,128)(2,1)S(1)}, bf16[1,64,32,128]{3,2,1,0:T(8,128)(2,1)}, u32[]{:S(2)}) copy-start(bf16[1,64,32,128]{3,2,1,0:T(8,128)(2,1)} %param.7) | copy-start | bytes 1572868
  24.6 15.4 %copy-start.16 = (s32[16]{0:T(128)S(1)}, s32[16]{0:T(128)}, u32[]{:S(2)}) copy-start(s32[16]{0:T(128)} %param.10) | copy-start | bytes 196
  26.4 23.4 %all-to-all-start = ((bf16[8,2,2048]{2,1,0:T(2,128)(2,1)}), bf16[8,2,2048]{2,1,0:T(2,128)(2,1)S(1)}, u32[]{:S(2)}, u32[]{:S(2)}) async-start(bf16[8,2,2048]{2,1,0:T(2,128)(2,1)} %reshape.455), calls=%async_computation | async-start | bytes 131072 | tf_op jit(solution)/shard_map/all_to_all | solution.py:119
  38.9 195.3 %all-reduce.3.cloned.1.call-start = ((), (), s32[]{:S(2)}) async-start(), calls=%async_computation.1 | async-start | bytes 1048576 | tf_op jit(solution)/shard_map/psum | solution.py:156
  51.0 3.3 %copy-start.11 = (f32[16,256]{1,0:T(8,128)S(1)}, f32[16,256]{1,0:T(8,128)}, u32[]{:S(2)}) copy-start(f32[16,256]{1,0:T(8,128)} %param.12) | copy-start | bytes 49156
  51.0 3.4 %copy-start.14 = (f32[16,256]{1,0:T(8,128)S(1)}, f32[16,256]{1,0:T(8,128)}, u32[]{:S(2)}) copy-start(f32[16,256]{1,0:T(8,128)} %param.11) | copy-start | bytes 49156
  51.0 3.5 %copy-start.9 = (s32[16,256]{1,0:T(8,128)S(1)}, s32[16,256]{1,0:T(8,128)}, u32[]{:S(2)}) copy-start(s32[16,256]{1,0:T(8,128)} %param.9) | copy-start | bytes 49156
  54.7 10.0 %collective-permute-start = (bf16[68,2,8,32]{3,2,1,0:T(8,128)(2,1)S(1)}, bf16[68,2,8,32]{3,2,1,0:T(8,128)(2,1)S(1)}, u32[]{:S(2)}, u32[]{:S(2)}) collective-permute-start(bf16[68,2,8,32]{3,2,1,0:T(8,128)(2,1)S(1)} %constant_dynamic-update-slice_fusion), channel_id=1, source_target_pairs={{0,8},{8,16},{16,24},{24,32},{32,40},{40,48},{48,56},{56,64},{64,7... | collective-permute-start | bytes 208904 | tf_op jit(solution)/shard_map/ppermute | solution.py:16
  56.6 9.8 %collective-permute-start.1 = (bf16[68,2,8,32]{3,2,1,0:T(8,128)(2,1)S(1)}, bf16[68,2,8,32]{3,2,1,0:T(8,128)(2,1)S(1)}, u32[]{:S(2)}, u32[]{:S(2)}) collective-permute-start(bf16[68,2,8,32]{3,2,1,0:T(8,128)(2,1)S(1)} %constant_dynamic-update-slice_fusion), channel_id=1, source_target_pairs={{8,0},{16,8},{24,16},{32,24},{40,32},{48,40},{56,48},{64,56},{72,6... | collective-permute-start | bytes 208904 | tf_op jit(solution)/shard_map/ppermute | solution.py:19
  66.4 8.3 %copy-start.1 = (bf16[68,2,8,32]{3,2,1,0:T(8,128)(2,1)}, bf16[68,2,8,32]{3,2,1,0:T(8,128)(2,1)S(1)}, u32[]{:S(2)}) copy-start(bf16[68,2,8,32]{3,2,1,0:T(8,128)(2,1)S(1)} %collective-permute-done.1) | copy-start | bytes 208900
  74.7 3.3 %copy-start.6 = (bf16[68,2,8,32]{3,2,1,0:T(8,128)(2,1)S(1)}, bf16[68,2,8,32]{3,2,1,0:T(8,128)(2,1)}, u32[]{:S(2)}) copy-start(bf16[68,2,8,32]{3,2,1,0:T(8,128)(2,1)} %get-tuple-element.15) | copy-start | bytes 208900
  85.4 4.5 %copy-start = (bf16[68,2,8,160]{3,2,1,0:T(8,128)(2,1)S(1)}, bf16[68,2,8,160]{3,2,1,0:T(8,128)(2,1)}, u32[]{:S(2)}) copy-start(bf16[68,2,8,160]{3,2,1,0:T(8,128)(2,1)} %concatenate.35) | copy-start | bytes 1044484
  86.5 6.4 %copy-start.4 = (bf16[64,2,8,160]{3,2,1,0:T(8,128)(2,1)}, bf16[64,2,8,160]{3,2,1,0:T(8,128)(2,1)S(1)}, u32[]{:S(2)}) copy-start(bf16[64,2,8,160]{3,2,1,0:T(8,128)(2,1)S(1)} %slice.239) | copy-start | bytes 983044
  88.1 2.0 copy-start.3
  90.1 1.0 copy-start.2
  90.8 1.1 copy-start.5
  92.5 1.7 copy-start.12
  92.9 2.6 copy-start.13
  92.9 142.6 %copy-start.10 = (f32[64,64]{1,0:T(8,128)S(1)}, f32[64,64]{1,0:T(8,128)}, u32[]{:S(2)}) copy-start(f32[64,64]{1,0:T(8,128)} %get-tuple-element.46) | copy-start | bytes 49156
  234.2 3.6 %copy-start.8 = (f32[16,64,64]{2,1,0:T(8,128)S(1)}, f32[16,64,64]{2,1,0:T(8,128)}, u32[]{:S(2)}) copy-start(f32[16,64,64]{2,1,0:T(8,128)} %all-reduce.3.cloned.1.call-done) | copy-start | bytes 786436
Sparse Core Ops, SparseCore 0:
  94.3 139.8 all-reduce.2
where the time goes:
time: 257 us; the launch traced here: 256 us
  waiting for transfers between devices  123 us (48%)
  local copies, waits for them, and re-layouts  41.4 us (16%)
  blocking collectives  26.8 us (10%)
  starting transfers between devices  20.4 us (8%)
  matrix products  16.5 us (6%)
  other arithmetic  14 us (5%)
  between operations  14 us (5%)
    psum x1, waiting for transfers between devices, shards(): gram_all, rhs_all = lax.psum((gram_flat, rhs_flat), 'lag')  112 us
    psum x1, blocking collectives, shards(): gram_all, rhs_all = lax.psum((gram_flat, rhs_flat), 'lag')  26.8 us
    gather x2, local copies, waits for them, and re-layouts, shards(): jnp.take(predicted_crowd_array.reshape(crowd_share_part, tile_vertical_ex...  13.6 us
    all_to_all x1, starting transfers between devices, shards(): lax.all_to_all(probed_markers, 'lag', split_axis=3, concat_axis=0, tiled=...  12.5 us
    concatenate x5, local copies, waits for them, and re-layouts, local_gram(): stacked = jnp.concatenate(pieces, axis=3)  8.81 us
    all_to_all x1, waiting for transfers between devices, shards(): lax.all_to_all(probed_markers, 'lag', split_axis=3, concat_axis=0, tiled=...  7.52 us
    ppermute x1, starting transfers between devices, padded_2(): lax.ppermute(lax.slice_in_dim(block, 0, width, axis=dim), axis, backward)  5.93 us
    unnamed x39, local copies, waits for them, and re-layouts  5.35 us
  transfers between devices with their start and end apart: 4, of which 4 were waited for; matrix products, arithmetic and copies ran while one was open for 2% of the time, Pallas kernels for 0%

commit v1 on v0

--- a/solution.py
+++ b/solution.py
@@ -116,7 +116,12 @@
         axis=1,
     )
     probed_markers = probed_markers.reshape(crowd_share_part, patch_rows, patch_cols, slot_count)
-    received = lax.all_to_all(probed_markers, "lag", split_axis=3, concat_axis=0, tiled=True)
+    received = jnp.concatenate(
+        lax.all_to_all(
+            jnp.stack(jnp.split(probed_markers, lax.axis_size("lag"), axis=3)), "lag", 0, 0
+        ),
+        axis=0,
+    )
     crowd_members_number = received.shape[0]
     average_reading = jnp.sum(received, axis=0, dtype=jnp.float32) / crowd_members_number
     obs_anomaly = (received.astype(jnp.float32) - average_reading).astype(jnp.bfloat16)

time: 257 us -> 249 us (0.969)
  other arithmetic: 14 us -> 9.9 us
  local copies, waits for them, and re-layouts: 41.4 us -> 37.7 us
    unnamed x39 -> x46, local copies, waits for them, and re-layouts: 5.35 us -> 4 us
where the time goes in v1:
time: 249 us
  waiting for transfers between devices  123 us (49%)
  local copies, waits for them, and re-layouts  37.7 us (15%)
  blocking collectives  26.8 us (11%)
  starting transfers between devices  20.4 us (8%)
  matrix products  16.5 us (7%)
  between operations  13.9 us (6%)
  other arithmetic  9.9 us (4%)
    psum x1, waiting for transfers between devices, shards(): gram_all, rhs_all = lax.psum((gram_flat, rhs_flat), 'lag')  112 us
    psum x1, blocking collectives, shards(): gram_all, rhs_all = lax.psum((gram_flat, rhs_flat), 'lag')  26.8 us
    all_to_all x1, starting transfers between devices, shards(): lax.all_to_all(jnp.stack(jnp.split(probed_markers, lax.axis_size('lag'),...  12.7 us
    gather x2, local copies, waits for them, and re-layouts, shards(): jnp.take(predicted_crowd_array.reshape(crowd_share_part, tile_vertical_ex...  12.5 us
    concatenate x5, local copies, waits for them, and re-layouts, local_gram(): stacked = jnp.concatenate(pieces, axis=3)  8.8 us
    all_to_all x1, waiting for transfers between devices, shards(): lax.all_to_all(jnp.stack(jnp.split(probed_markers, lax.axis_size('lag'),...  7.59 us
    ppermute x1, starting transfers between devices, padded_2(): lax.ppermute(lax.slice_in_dim(block, 0, width, axis=dim), axis, backward)  5.75 us
  transfers between devices with their start and end apart: 4, of which 4 were waited for; matrix products, arithmetic and copies ran while one was open for 2% of the time, Pallas kernels for 0%

profile of v1, /device:TPU:2, one launch (start us, length us, event | category | flops | bytes accessed | tf_op | source)
XLA Modules:
  0.0 248.7 jit_solution(9822094062889660259)
XLA Ops:
  7.5 1.3 copy.117
  8.8 12.1 %gather_fusion = bf16[4096,8]{1,0:T(8,128)(2,1)S(1)} fusion(bf16[8,4096]{0,1:T(8,128)(2,1)S(1)} %bitcast.352, s32[4096]{0:T(1024)S(1)} %broadcast_clamp_fusion), kind=kCustom, calls=%fused_computation | custom fusion | bytes 147456 | tf_op jit(solution)/shard_map/jit(_take)/gather | solution.py:113
  22.8 12.7 %all-to-all-start = ((bf16[8,2,2048]{2,1,0:T(2,128)(2,1)}), bf16[8,2,2048]{2,1,0:T(2,128)(2,1)S(1)}, u32[]{:S(2)}, u32[]{:S(2)}) async-start(bf16[8,2,2048]{2,1,0:T(2,128)(2,1)} %reshape.451), calls=%async_computation | async-start | bytes 131072 | tf_op jit(solution)/shard_map/all_to_all | solution.py:120
  38.8 7.6 %all-to-all-done = bf16[8,2,2048]{2,1,0:T(2,128)(2,1)S(1)} async-done(((bf16[8,2,2048]{2,1,0:T(2,128)(2,1)}), bf16[8,2,2048]{2,1,0:T(2,128)(2,1)S(1)}, u32[]{:S(2)}, u32[]{:S(2)}) %all-to-all-start) | async-done | bytes 65568 | tf_op jit(solution)/shard_map/all_to_all | solution.py:120
  47.1 1.9 collective-permute-start
  49.0 5.8 %collective-permute-start.1 = (bf16[68,2,8,32]{3,2,1,0:T(8,128)(2,1)S(1)}, bf16[68,2,8,32]{3,2,1,0:T(8,128)(2,1)S(1)}, u32[]{:S(2)}, u32[]{:S(2)}) collective-permute-start(bf16[68,2,8,32]{3,2,1,0:T(8,128)(2,1)S(1)} %constant_dynamic-update-slice_fusion), channel_id=1, source_target_pairs={{8,0},{16,8},{24,16},{32,24},{40,32},{48,40},{56,48},{64,56},{72,6... | collective-permute-start | bytes 208904 | tf_op jit(solution)/shard_map/ppermute | solution.py:19
  54.8 2.3 collective-permute-done
  57.0 1.8 collective-permute-done.1
  59.6 2.8 %fusion.173 = (bf16[68,2,8,32]{3,2,1,0:T(8,128)(2,1)}, bf16[68,2,8,32]{3,2,1,0:T(8,128)(2,1)}, bf16[68,2,8,32]{3,2,1,0:T(8,128)(2,1)}, bf16[68,2,8,32]{3,2,1,0:T...) fusion(bf16[68,6,12,32]{3,2,1,0:T(8,128)(2,1)S(1)} %fusion.5), kind=kLoop, calls=%fused_computation.269 | loop fusion | bytes 2646016 | tf_op jit(solution)/shard_map/slice | solution.py:58
  64.9 1.6 concatenate.29
  68.0 1.6 concatenate.31
  70.5 1.5 concatenate.32
  72.9 1.7 concatenate.34
  75.4 2.4 concatenate.35
  77.8 1.1 slice.239
  78.9 1.6 fusion.165
  85.4 1.2 convolution_add_fusion
  86.6 1.3 fusion.23
  87.9 26.8 %psum.15 = f32[16,64]{1,0:T(8,128)S(1)} all-reduce(f32[16,64]{1,0:T(8,128)S(1)} %add_bitcast_fusion), channel_id=1, replica_groups=mesh['dom'=64,'lag'=8] {'lag'}, use_global_device_ids=true, to_apply=%region_3.4 | all-reduce | flops 1024 | bytes 8192 | tf_op jit(solution)/shard_map/psum | solution.py:161
  114.7 111.8 %all-reduce.3.cloned.1.call-done = f32[16,64,64]{2,1,0:T(8,128)} async-done(((f32[16,64,64]{2,1,0:T(8,128)}), f32[16,64,64]{2,1,0:T(8,128)}) %all-reduce.3.cloned.1.call-update) | async-done | bytes 262160 | tf_op jit(solution)/shard_map/psum | solution.py:161
  226.5 1.3 multiply_reduce_fusion
  227.8 1.7 fusion.9
  237.0 0.9 fusion.179
  240.2 1.6 copy.138
  (116 shorter events, 28.3 us)
Async XLA Ops:
  6.5 29.0 %copy-start.15 = (s32[16]{0:T(128)S(1)}, s32[16]{0:T(128)}, u32[]{:S(2)}) copy-start(s32[16]{0:T(128)} %param.13) | copy-start | bytes 196
  6.5 29.0 %copy-start.7 = (bf16[1,64,32,128]{3,2,1,0:T(8,128)(2,1)S(1)}, bf16[1,64,32,128]{3,2,1,0:T(8,128)(2,1)}, u32[]{:S(2)}) copy-start(bf16[1,64,32,128]{3,2,1,0:T(8,128)(2,1)} %param.7) | copy-start | bytes 1572868
  21.3 15.4 %copy-start.16 = (s32[16]{0:T(128)S(1)}, s32[16]{0:T(128)}, u32[]{:S(2)}) copy-start(s32[16]{0:T(128)} %param.10) | copy-start | bytes 196
  22.8 23.9 %copy-start.11 = (f32[16,256]{1,0:T(8,128)S(1)}, f32[16,256]{1,0:T(8,128)}, u32[]{:S(2)}) copy-start(f32[16,256]{1,0:T(8,128)} %param.12) | copy-start | bytes 49156
  22.8 24.0 %copy-start.14 = (f32[16,256]{1,0:T(8,128)S(1)}, f32[16,256]{1,0:T(8,128)}, u32[]{:S(2)}) copy-start(f32[16,256]{1,0:T(8,128)} %param.11) | copy-start | bytes 49156
  22.8 24.1 %copy-start.9 = (s32[16,256]{1,0:T(8,128)S(1)}, s32[16,256]{1,0:T(8,128)}, u32[]{:S(2)}) copy-start(s32[16,256]{1,0:T(8,128)} %param.9) | copy-start | bytes 49156
  22.8 23.6 %all-to-all-start = ((bf16[8,2,2048]{2,1,0:T(2,128)(2,1)}), bf16[8,2,2048]{2,1,0:T(2,128)(2,1)S(1)}, u32[]{:S(2)}, u32[]{:S(2)}) async-start(bf16[8,2,2048]{2,1,0:T(2,128)(2,1)} %reshape.451), calls=%async_computation | async-start | bytes 131072 | tf_op jit(solution)/shard_map/all_to_all | solution.py:120
  35.4 191.1 %all-reduce.3.cloned.1.call-start = ((), (), s32[]{:S(2)}) async-start(), calls=%async_computation.1 | async-start | bytes 1048576 | tf_op jit(solution)/shard_map/psum | solution.py:161
  47.1 10.0 %collective-permute-start = (bf16[68,2,8,32]{3,2,1,0:T(8,128)(2,1)S(1)}, bf16[68,2,8,32]{3,2,1,0:T(8,128)(2,1)S(1)}, u32[]{:S(2)}, u32[]{:S(2)}) collective-permute-start(bf16[68,2,8,32]{3,2,1,0:T(8,128)(2,1)S(1)} %constant_dynamic-update-slice_fusion), channel_id=1, source_target_pairs={{0,8},{8,16},{16,24},{24,32},{32,40},{40,48},{48,56},{56,64},{64,7... | collective-permute-start | bytes 208904 | tf_op jit(solution)/shard_map/ppermute | solution.py:16
  49.0 9.8 %collective-permute-start.1 = (bf16[68,2,8,32]{3,2,1,0:T(8,128)(2,1)S(1)}, bf16[68,2,8,32]{3,2,1,0:T(8,128)(2,1)S(1)}, u32[]{:S(2)}, u32[]{:S(2)}) collective-permute-start(bf16[68,2,8,32]{3,2,1,0:T(8,128)(2,1)S(1)} %constant_dynamic-update-slice_fusion), channel_id=1, source_target_pairs={{8,0},{16,8},{24,16},{32,24},{40,32},{48,40},{56,48},{64,56},{72,6... | collective-permute-start | bytes 208904 | tf_op jit(solution)/shard_map/ppermute | solution.py:19
  58.8 8.4 %copy-start.1 = (bf16[68,2,8,32]{3,2,1,0:T(8,128)(2,1)}, bf16[68,2,8,32]{3,2,1,0:T(8,128)(2,1)S(1)}, u32[]{:S(2)}) copy-start(bf16[68,2,8,32]{3,2,1,0:T(8,128)(2,1)S(1)} %collective-permute-done.1) | copy-start | bytes 208900
  67.2 3.3 %copy-start.6 = (bf16[68,2,8,32]{3,2,1,0:T(8,128)(2,1)S(1)}, bf16[68,2,8,32]{3,2,1,0:T(8,128)(2,1)}, u32[]{:S(2)}) copy-start(bf16[68,2,8,32]{3,2,1,0:T(8,128)(2,1)} %get-tuple-element.17) | copy-start | bytes 208900
  77.8 4.5 %copy-start = (bf16[68,2,8,160]{3,2,1,0:T(8,128)(2,1)S(1)}, bf16[68,2,8,160]{3,2,1,0:T(8,128)(2,1)}, u32[]{:S(2)}) copy-start(bf16[68,2,8,160]{3,2,1,0:T(8,128)(2,1)} %concatenate.35) | copy-start | bytes 1044484
  78.9 6.4 %copy-start.4 = (bf16[64,2,8,160]{3,2,1,0:T(8,128)(2,1)}, bf16[64,2,8,160]{3,2,1,0:T(8,128)(2,1)S(1)}, u32[]{:S(2)}) copy-start(bf16[64,2,8,160]{3,2,1,0:T(8,128)(2,1)S(1)} %slice.239) | copy-start | bytes 983044
  80.6 2.0 copy-start.3
  82.5 1.0 copy-start.2
  83.3 1.1 copy-start.5
  84.9 1.7 copy-start.12
  85.4 2.6 %copy-start.13 = (f32[2,8,1,64]{3,2,1,0:T(1,128)S(1)}, f32[2,8,1,64]{3,2,1,0:T(1,128)}, u32[]{:S(2)}) copy-start(f32[2,8,1,64]{3,2,1,0:T(1,128)} %fusion.21) | copy-start | bytes 12292
  85.4 142.5 %copy-start.10 = (f32[64,64]{1,0:T(8,128)S(1)}, f32[64,64]{1,0:T(8,128)}, u32[]{:S(2)}) copy-start(f32[64,64]{1,0:T(8,128)} %get-tuple-element.48) | copy-start | bytes 49156
  226.5 3.6 %copy-start.8 = (f32[16,64,64]{2,1,0:T(8,128)S(1)}, f32[16,64,64]{2,1,0:T(8,128)}, u32[]{:S(2)}) copy-start(f32[16,64,64]{2,1,0:T(8,128)} %all-reduce.3.cloned.1.call-done) | copy-start | bytes 786436
Sparse Core Ops, SparseCore 0:
  86.7 139.7 all-reduce.2
